TPU v7x, 256 devices: a whole 4x4x8 slice. The times are simulated.
256 devices in a mesh: drive: 4 (over y), brick: 64 (over x, z, core).
Axes of the slice: x: 4, y: 4, z: 8, core: 2. Of those that a mesh axis runs over, the one named last changes fastest.
Arguments:
- cam_tiles: bfloat16 [4, 1, 256, 64, 256], P('drive', None, 'brick')
- vox_embed: bfloat16 [1536, 128, 256], P('brick'), may hold values from -6 to 6
- prev_state: bfloat16 [4, 1536, 128, 256], P('drive', 'brick'), may hold values from -6 to 6
- tile_sends: int32 [4, 1, 64, 128], P('drive', None, 'brick'), may hold values from 0 to 3, as said below
- brick_tiles: int32 [4, 1, 1536, 8], P('drive', None, 'brick'), may hold values from -1 to 127, as said below
- ego_shift: int32 [4, 1], P('drive'), may hold values from 0 to 24
- norm_gains: float32 [2, 256], replicated, may hold values from 0.1 to 1.9
- w_query: bfloat16 [256, 256], replicated, may hold values from -0.375 to 0.375
- w_keyval: bfloat16 [256, 512], replicated, may hold values from -0.375 to 0.375
- w_attn_out: bfloat16 [256, 256], replicated, may hold values from -0.375 to 0.375
- w_in: bfloat16 [256, 512], replicated, may hold values from -0.375 to 0.375
- w_out: bfloat16 [512, 256], replicated, may hold values from -0.25 to 0.25
- grad_out: bfloat16 [4, 1536, 128, 256], P('drive', 'brick'), may hold values from -0.015625 to 0.015625
Outputs:
- new_state: bfloat16 [4, 1536, 128, 256], P('drive', 'brick')
- grad_w_in: float32 [256, 512], replicated
- grad_w_out: float32 [512, 256], replicated
Inputs may be any that keep to these rules, and one draw needn't show every extreme that they name: `tile_sends`: entry [drive, frame, p, d * 2 + c] is a tile of shard p, a local index, that shard p sends to shard d as its c-th slot; the 2 entries of one pair are distinct. `brick_tiles`: -1 is padding; other entries are distinct within a brick and name received slots; every brick has one or more, and in each drive and frame some brick has all 8.
All inputs are finite; a program needn't handle non-finite values.
Results may differ from a plain program's by a relative error of at most 0.0022.
The roundings to bfloat16 on the way count: a program that leaves them out, or rounds other values in their place, can miss the bound.
Values may be sent and summed in bfloat16 or wider, within the bound.
No kernel may reach another device: no remote copies, remote signals or barrier semaphores. Data moves between devices by JAX's collectives and lax.ppermute only.
A program may use at most 128 MiB of HBM per device.

v0:
```python
import jax
import jax.numpy as jnp
from jax import lax
from jax.sharding import PartitionSpec as P

HD = 32


def passed_along(value, axis, by):
    count = lax.axis_size(axis)
    pairs = [(i, i + by) for i in range(count) if 0 <= i + by < count]
    return lax.ppermute(value, axis, pairs)


def rms_norm(values, norm_gain):
    mean_sq = jnp.mean(values * values, axis=-1, keepdims=True)
    return values * lax.rsqrt(mean_sq + 1e-06) * norm_gain


def gelu_tanh(values):
    return jax.nn.gelu(values, approximate=True)


def take_rows(source_rows, positions):
    return source_rows[positions]


def on_device(
    cam_tiles,
    vox_embed,
    prev_state,
    tile_sends,
    brick_tiles,
    ego_shift,
    norm_gains,
    w_query,
    w_keyval,
    w_attn_out,
    w_in,
    w_out,
    grad_out,
):
    shards = lax.axis_size("brick")
    own_index = lax.axis_index("brick")
    frames = cam_tiles.shape[1]
    tile_dev = cam_tiles.shape[2]
    pixels = cam_tiles.shape[3]
    width = cam_tiles.shape[4]
    slots = tile_sends.shape[3]
    capacity = slots // shards
    brick_dev = vox_embed.shape[0]
    brick_size = vox_embed.shape[1]
    list_len = brick_tiles.shape[3]
    head_count = width // HD
    scale = 1.0 / HD**0.5
    group_size = min(brick_dev, max(1, 512 // brick_size))
    blocks = brick_dev // group_size
    tile_feats = cam_tiles[0]
    payload = (
        jnp.dot(tile_feats.reshape(-1, width), w_keyval, preferred_element_type=jnp.float32)
        .astype(jnp.bfloat16)
        .reshape(frames, tile_dev, pixels, 2 * width)
    )
    everything, all_plans = (
        lax.all_gather(payload, "brick", axis=1, tiled=True),
        lax.all_gather(tile_sends[0], "brick", axis=1, tiled=True),
    )
    own_plan = lax.dynamic_slice_in_dim(all_plans, own_index * capacity, capacity, 2)
    slot_index = (jnp.arange(shards, dtype=jnp.int32)[:, None] * tile_dev + own_plan).reshape(
        frames, slots
    )
    slot_data = jax.vmap(take_rows)(everything, slot_index)
    voxel_state = prev_state[0]
    behind = passed_along(voxel_state, "brick", 1)
    joined = jnp.concatenate([behind, voxel_state], 0)
    start = brick_dev - ego_shift[0, 0]
    shifted = lax.dynamic_slice_in_dim(joined, start, brick_dev, 0)
    q_in = vox_embed.astype(jnp.float32) + shifted.astype(jnp.float32)
    normed = rms_norm(q_in, norm_gains[0]).astype(jnp.bfloat16)
    queries = jnp.dot(
        normed.reshape(-1, width), w_query, preferred_element_type=jnp.float32
    ).astype(jnp.bfloat16)
    query_blocks = queries.reshape(blocks, group_size, brick_size, head_count, HD)
    keyval = slot_data[0]
    entries = brick_tiles[0, 0]

    def attend(operands):
        query_block, entry_block = operands
        gathered = keyval[jnp.maximum(entry_block, 0)].reshape(
            group_size, list_len * pixels, 2, head_count, HD
        )
        keys_part = gathered[:, :, 0]
        values_part = gathered[:, :, 1]
        scores = (
            jnp.einsum(
                "gqhd,gkhd->ghqk", query_block, keys_part, preferred_element_type=jnp.float32
            )
            * scale
        )
        live_keys = jnp.broadcast_to(
            (entry_block >= 0)[:, :, None], (group_size, list_len, pixels)
        ).reshape(group_size, 1, 1, list_len * pixels)
        scores = jnp.where(live_keys, scores, -1e30)
        row_peak = jnp.max(scores, axis=-1, keepdims=True)
        raised = jnp.exp(scores - row_peak)
        weights = (raised / jnp.sum(raised, axis=-1, keepdims=True)).astype(jnp.bfloat16)
        mixed = jnp.einsum(
            "ghqk,gkhd->gqhd", weights, values_part, preferred_element_type=jnp.float32
        )
        return mixed.astype(jnp.bfloat16)

    attended = lax.map(
        attend, (query_blocks, entries.reshape(blocks, group_size, list_len))
    ).reshape(-1, width)
    residual_x = q_in.reshape(-1, width) + jnp.dot(
        attended, w_attn_out, preferred_element_type=jnp.float32
    )
    hidden_in = rms_norm(residual_x, norm_gains[1]).astype(jnp.bfloat16)
    pre_act = jnp.dot(hidden_in, w_in, preferred_element_type=jnp.float32)
    activated = gelu_tanh(pre_act).astype(jnp.bfloat16)
    voxel_state = (
        (residual_x + jnp.dot(activated, w_out, preferred_element_type=jnp.float32))
        .astype(jnp.bfloat16)
        .reshape(brick_dev, brick_size, width)
    )
    cotangent = grad_out[0].reshape(-1, width)
    part_w_out = jnp.dot(activated.T, cotangent, preferred_element_type=jnp.float32)
    d_act = jnp.dot(cotangent, w_out.T, preferred_element_type=jnp.float32)
    unused_value, pullback = jax.vjp(gelu_tanh, pre_act)
    d_pre = pullback(d_act)[0].astype(jnp.bfloat16)
    part_w_in = jnp.dot(hidden_in.T, d_pre, preferred_element_type=jnp.float32)
    grad_w_in, grad_w_out = lax.psum((part_w_in, part_w_out), ("drive", "brick"))
    return (voxel_state[None], grad_w_in, grad_w_out)


def solution(mesh):
    return jax.shard_map(
        on_device,
        mesh=mesh,
        in_specs=(
            P("drive", None, "brick", None, None),
            P("brick", None, None),
            P("drive", "brick", None, None),
            P("drive", None, "brick", None),
            P("drive", None, "brick", None),
            P("drive", None),
            P(),
            P(),
            P(),
            P(),
            P(),
            P(),
            P("drive", "brick", None, None),
        ),
        out_specs=(P("drive", "brick", None, None), P(), P()),
        check_vma=False,
    )
```

profile of v0, /device:TPU:2, one launch (start us, length us, event | category | flops | bytes accessed | tf_op | source)
XLA Modules:
  0.0 652.4 jit_solution(17826369599442796199)
XLA Ops:
  11.9 58.8 %all-gather = s32[1,64,1,128]{3,2,0,1:T(1,128)S(1)} all-gather(s32[1,1,1,128]{3,2,0,1:T(1,128)} %bitcast.78), channel_id=2, replica_groups=mesh['drive'=4,'brick'=64] {'brick'}, dimensions={1}, use_global_device_ids=true | all-gather | bytes 33280 | tf_op jit(solution)/shard_map/all_gather | solution.py:66
  84.6 28.0 %all-gather.3.cloned.1.call-done = bf16[1,256,64,512]{3,2,0,1:T(8,128)(2,1)} async-done(((bf16[1,4,64,512]{3,2,0,1:T(8,128)(2,1)}), bf16[1,256,64,512]{3,2,0,1:T(8,128)(2,1)}) %all-gather.3.cloned.1.call-update) | async-done | bytes 16777232 | tf_op jit(solution)/shard_map/all_gather | solution.py:65
  112.7 12.5 %gather_fusion.1 = bf16[128,64,512]{2,1,0:T(8,128)(2,1)} fusion(bf16[1,256,64,512]{3,2,0,1:T(8,128)(2,1)} %all-gather.3.cloned.1.call-done, s32[128]{0:T(128)S(1)} %or_bitcast_fusion), kind=kCustom, calls=%fused_computation.1 | custom fusion | bytes 16778240 | tf_op jit(solution)/shard_map/vmap()/gather | solution.py:25
  125.2 235.8 %while.10 = (s32[]{:T(128)}, bf16[6,4,128,8,32]{2,1,0,4,3:T(4,128)(2,1)}, s32[6,4,8]{2,1,0:T(4,128)S(1)}, bf16[128,64,512]{2,1,0:T(8,128)(2,1)}, bf16[6,4,128,8,32]{2,1,0,4,3:T(4,128)(2,1)}, /*index=5*/s32[]{:T(128)}) while((s32[]{:T(128)}, bf16[6,4,128,8,32]{2,1,0,4,3:T(4,128)(2,1)}, s32[6,4,8]{2,1,0:T(4,128)S(1)}, ...), condition=%wide.region_4.5_spmd, body=%wide.region_1.4_spmd.sunk | while | flops 285345344 | bytes 54048272 | solution.py:112
  130.6 7.4 %copy.61 = bf16[32,64,512]{1,0,2:T(8,128)(2,1)} copy(bf16[32,64,512]{2,1,0:T(8,128)(2,1)} %gather_fusion) | data formatting | bytes 4194304 | tf_op jit(solution)/shard_map/while/body/eval_jaxpr/gather | solution.py:89
  138.1 6.7 %reshape.153 = bf16[4,512,2,8,32]{1,0,4,3,2:T(4,128)(2,1)} reshape(bf16[32,64,512]{1,0,2:T(8,128)(2,1)} %copy.61) | data formatting | bytes 4194304 | tf_op jit(solution)/shard_map/while/body/eval_jaxpr/reshape | solution.py:89
  152.8 8.7 %fusion.54 = (f32[4,8,128]{2,1,0:T(8,128)S(1)}, f32[4,8,128,512]{3,2,1,0:T(8,128)S(1)}) fusion(f32[4,8,128,512]{3,2,1,0:T(8,128)} %fusion.53, pred[4,512]{1,0:T(4,128)(4,1)S(1)} %broadcast_in_dim.57), kind=kOutput, calls=%fused_computation.65.clone.1 | output fusion | flops 12583423 | bytes 16795648 | tf_op jit(solution)/shard_map/while/body/eval_jaxpr/sub | solution.py:105
  169.9 7.4 %copy.61 = bf16[32,64,512]{1,0,2:T(8,128)(2,1)} copy(bf16[32,64,512]{2,1,0:T(8,128)(2,1)} %gather_fusion) | data formatting | bytes 4194304 | tf_op jit(solution)/shard_map/while/body/eval_jaxpr/gather | solution.py:89
  177.3 6.7 %reshape.153 = bf16[4,512,2,8,32]{1,0,4,3,2:T(4,128)(2,1)} reshape(bf16[32,64,512]{1,0,2:T(8,128)(2,1)} %copy.61) | data formatting | bytes 4194304 | tf_op jit(solution)/shard_map/while/body/eval_jaxpr/reshape | solution.py:89
  192.1 8.7 %fusion.54 = (f32[4,8,128]{2,1,0:T(8,128)S(1)}, f32[4,8,128,512]{3,2,1,0:T(8,128)S(1)}) fusion(f32[4,8,128,512]{3,2,1,0:T(8,128)} %fusion.53, pred[4,512]{1,0:T(4,128)(4,1)S(1)} %broadcast_in_dim.57), kind=kOutput, calls=%fused_computation.65.clone.1 | output fusion | flops 12583423 | bytes 16795648 | tf_op jit(solution)/shard_map/while/body/eval_jaxpr/sub | solution.py:105
  209.2 7.4 %copy.61 = bf16[32,64,512]{1,0,2:T(8,128)(2,1)} copy(bf16[32,64,512]{2,1,0:T(8,128)(2,1)} %gather_fusion) | data formatting | bytes 4194304 | tf_op jit(solution)/shard_map/while/body/eval_jaxpr/gather | solution.py:89
  216.6 6.7 %reshape.153 = bf16[4,512,2,8,32]{1,0,4,3,2:T(4,128)(2,1)} reshape(bf16[32,64,512]{1,0,2:T(8,128)(2,1)} %copy.61) | data formatting | bytes 4194304 | tf_op jit(solution)/shard_map/while/body/eval_jaxpr/reshape | solution.py:89
  231.4 8.7 %fusion.54 = (f32[4,8,128]{2,1,0:T(8,128)S(1)}, f32[4,8,128,512]{3,2,1,0:T(8,128)S(1)}) fusion(f32[4,8,128,512]{3,2,1,0:T(8,128)} %fusion.53, pred[4,512]{1,0:T(4,128)(4,1)S(1)} %broadcast_in_dim.57), kind=kOutput, calls=%fused_computation.65.clone.1 | output fusion | flops 12583423 | bytes 16795648 | tf_op jit(solution)/shard_map/while/body/eval_jaxpr/sub | solution.py:105
  248.5 7.4 %copy.61 = bf16[32,64,512]{1,0,2:T(8,128)(2,1)} copy(bf16[32,64,512]{2,1,0:T(8,128)(2,1)} %gather_fusion) | data formatting | bytes 4194304 | tf_op jit(solution)/shard_map/while/body/eval_jaxpr/gather | solution.py:89
  255.9 6.7 %reshape.153 = bf16[4,512,2,8,32]{1,0,4,3,2:T(4,128)(2,1)} reshape(bf16[32,64,512]{1,0,2:T(8,128)(2,1)} %copy.61) | data formatting | bytes 4194304 | tf_op jit(solution)/shard_map/while/body/eval_jaxpr/reshape | solution.py:89
  270.7 8.7 %fusion.54 = (f32[4,8,128]{2,1,0:T(8,128)S(1)}, f32[4,8,128,512]{3,2,1,0:T(8,128)S(1)}) fusion(f32[4,8,128,512]{3,2,1,0:T(8,128)} %fusion.53, pred[4,512]{1,0:T(4,128)(4,1)S(1)} %broadcast_in_dim.57), kind=kOutput, calls=%fused_computation.65.clone.1 | output fusion | flops 12583423 | bytes 16795648 | tf_op jit(solution)/shard_map/while/body/eval_jaxpr/sub | solution.py:105
  287.8 7.4 %copy.61 = bf16[32,64,512]{1,0,2:T(8,128)(2,1)} copy(bf16[32,64,512]{2,1,0:T(8,128)(2,1)} %gather_fusion) | data formatting | bytes 4194304 | tf_op jit(solution)/shard_map/while/body/eval_jaxpr/gather | solution.py:89
  295.2 6.7 %reshape.153 = bf16[4,512,2,8,32]{1,0,4,3,2:T(4,128)(2,1)} reshape(bf16[32,64,512]{1,0,2:T(8,128)(2,1)} %copy.61) | data formatting | bytes 4194304 | tf_op jit(solution)/shard_map/while/body/eval_jaxpr/reshape | solution.py:89
  310.0 8.7 %fusion.54 = (f32[4,8,128]{2,1,0:T(8,128)S(1)}, f32[4,8,128,512]{3,2,1,0:T(8,128)S(1)}) fusion(f32[4,8,128,512]{3,2,1,0:T(8,128)} %fusion.53, pred[4,512]{1,0:T(4,128)(4,1)S(1)} %broadcast_in_dim.57), kind=kOutput, calls=%fused_computation.65.clone.1 | output fusion | flops 12583423 | bytes 16795648 | tf_op jit(solution)/shard_map/while/body/eval_jaxpr/sub | solution.py:105
  327.1 7.4 %copy.61 = bf16[32,64,512]{1,0,2:T(8,128)(2,1)} copy(bf16[32,64,512]{2,1,0:T(8,128)(2,1)} %gather_fusion) | data formatting | bytes 4194304 | tf_op jit(solution)/shard_map/while/body/eval_jaxpr/gather | solution.py:89
  334.5 6.7 %reshape.153 = bf16[4,512,2,8,32]{1,0,4,3,2:T(4,128)(2,1)} reshape(bf16[32,64,512]{1,0,2:T(8,128)(2,1)} %copy.61) | data formatting | bytes 4194304 | tf_op jit(solution)/shard_map/while/body/eval_jaxpr/reshape | solution.py:89
  349.3 8.7 %fusion.54 = (f32[4,8,128]{2,1,0:T(8,128)S(1)}, f32[4,8,128,512]{3,2,1,0:T(8,128)S(1)}) fusion(f32[4,8,128,512]{3,2,1,0:T(8,128)} %fusion.53, pred[4,512]{1,0:T(4,128)(4,1)S(1)} %broadcast_in_dim.57), kind=kOutput, calls=%fused_computation.65.clone.1 | output fusion | flops 12583423 | bytes 16795648 | tf_op jit(solution)/shard_map/while/body/eval_jaxpr/sub | solution.py:105
  374.7 9.6 %fusion.19 = f32[256,512]{1,0:T(8,128)} fusion(f32[3072,512]{1,0:T(8,128)} %get-tuple-element.69, bf16[3072,256]{1,0:T(8,128)(2,1)S(1)} %bitcast.65, bf16[512,256]{1,0:T(8,128)(2,1)S(1)} %copy-done.4, f32[3072,256]{1,0:T(8,128)} %copy-done.2, f32[256]{0:T(256)S(1)} %bitcast.77, f32[3072]{0:T(1024)S(1)} %add_rsqrt_fusion), kind=kOutput, calls=%fused_computation.45 | convolution fusion | flops 1644429312 | bytes 11809792 | tf_op jit(solution)/shard_map/dot_general | solution.py:131
  389.3 252.5 %all-reduce.3.cloned.1.call-done = (f32[256,512]{1,0:T(8,128)}, f32[512,256]{1,0:T(8,128)}) async-done(((f32[256,512]{1,0:T(8,128)}, f32[512,256]{1,0:T(8,128)}), (f32[256,512]{1,0:T(8,128)}, f32[512,256]{1,0:T(8,128)})) %all-reduce.3.cloned.1.call-update) | async-done | bytes 1048592 | tf_op jit(solution)/shard_map/psum | solution.py:132
  (121 shorter events, 138.7 us)
Async XLA Ops:
  7.2 364.0 %copy-start = (bf16[1,24,128,256]{3,2,1,0:T(8,128)(2,1)S(1)}, bf16[1,24,128,256]{3,2,1,0:T(8,128)(2,1)}, u32[]{:S(2)}) copy-start(bf16[1,24,128,256]{3,2,1,0:T(8,128)(2,1)} %param.27) | copy-start | bytes 4718596
  7.2 105.5 %all-gather.3.cloned.1.call-start = ((), (), s32[]{:S(2)}) async-start(), calls=%async_computation | async-start | bytes 17039360 | tf_op jit(solution)/shard_map/all_gather | solution.py:65
  9.3 632.6 %all-reduce.3.cloned.1.call-start = ((), (), s32[]{:S(2)}) async-start(), calls=%async_computation.1 | async-start | bytes 2097152 | tf_op jit(solution)/shard_map/psum | solution.py:132
  9.3 63.4 %collective-permute-start = (bf16[24,128,256]{2,1,0:T(8,128)(2,1)}, bf16[24,128,256]{2,1,0:T(8,128)(2,1)S(1)}, u32[]{:S(2)}, u32[]{:S(2)}) collective-permute-start(bf16[24,128,256]{2,1,0:T(8,128)(2,1)} %bitcast.70), channel_id=1, source_target_pairs={{0,1},{1,2},{2,3},{3,4},{4,5},{5,6},{6,7},{7,8},{8,9},{9,10},{10,1... | collective-permute-start | bytes 4718600 | tf_op jit(solution)/shard_map/ppermute | solution.py:12
  75.6 1.7 copy-start.1
  75.7 2.2 copy-start.6
  360.9 2.9 copy-start.5
  363.8 3.1 copy-start.7
  366.8 4.4 copy-start.2
  371.2 1.7 copy-start.3
  371.2 3.5 copy-start.4
Sparse Core Ops, SparseCore 0:
  11.3 101.2 all-gather.2
  384.5 257.3 all-reduce.2
where the time goes:
time: 655 us; the launch traced here: 652 us
  waiting for transfers between devices  281 us (43%)
  local copies, waits for them, and re-layouts  175 us (27%)
  matrix products  65.4 us (10%)
  blocking collectives  58.8 us (9%)
  other arithmetic  55.9 us (9%)
  between operations  14.8 us (2%)
    psum x1, waiting for transfers between devices, on_device(): lax.psum((part_w_in, part_w_out), ('drive', 'brick'))  253 us
    gather x12, local copies, waits for them, and re-layouts, attend(): keyval[jnp.maximum(entry_block, 0)]  76.8 us
    all_gather x1, blocking collectives, on_device(): lax.all_gather(tile_sends[0], 'brick', axis=1, tiled=True)  58.8 us
    sub x6, other arithmetic, attend(): raised = jnp.exp(scores - row_peak)  52.4 us
    reshape x6, local copies, waits for them, and re-layouts, attend(): keyval[jnp.maximum(entry_block, 0)]  40.4 us
    all_gather x1, waiting for transfers between devices, on_device(): lax.all_gather(payload, 'brick', axis=1, tiled=True)  28 us
    dot_general x6, matrix products, attend(): jnp.einsum('gqhd,gkhd->ghqk', query_block, keys_part, preferred_element_t...  27.2 us
    slice x6, local copies, waits for them, and re-layouts, attend(): values_part = gathered[:, :, 1]  13.6 us
  transfers between devices with their start and end apart: 3, of which 2 were waited for; matrix products, arithmetic and copies ran while one was open for 3% of the time, Pallas kernels for 0%

commit v1 on v0

--- a/solution.py
+++ b/solution.py
@@ -62,7 +62,9 @@
         .reshape(frames, tile_dev, pixels, 2 * width)
     )
     everything, all_plans = (
-        lax.all_gather(payload, "brick", axis=1, tiled=True),
+        jnp.concatenate(
+            lax.all_to_all(jnp.stack([payload] * lax.axis_size("brick")), "brick", 0, 0), axis=1
+        ),
         lax.all_gather(tile_sends[0], "brick", axis=1, tiled=True),
     )
     own_plan = lax.dynamic_slice_in_dim(all_plans, own_index * capacity, capacity, 2)

time: 655 us -> 989 us (1.51)
  blocking collectives: 58.8 us -> 404 us
  waiting for transfers between devices: 281 us -> 253 us
  starting transfers between devices: 2 us -> 14.4 us
    all_gather x1, blocking collectives: 58.8 us -> 404 us  [on_device(): lax.all_gather(tile_sends[0], 'brick', axis=1, tiled=True)]
    all_gather x1 -> x0, waiting for transfers between devices: 28 us -> none  [on_device(): lax.all_gather(payload, 'brick', axis=1, tiled=True)]
    all_to_all x0 -> x1, starting transfers between devices: none -> 12.4 us  [on_device(): lax.all_to_all(jnp.stack([payload] * lax.axis_size('brick')), 'brick', 0, 0)]
  transfers between devices with their start and end apart: 3 -> 3, of which waited for: 2 -> 1; matrix products, arithmetic and copies ran while one was open for 3% -> 2% of each run, Pallas kernels for 0% -> 0%
where the time goes in v1:
time: 989 us; the launch traced here: 987 us
  blocking collectives  404 us (41%)
  waiting for transfers between devices  253 us (26%)
  local copies, waits for them, and re-layouts  180 us (18%)
  matrix products  64.6 us (7%)
  other arithmetic  55.7 us (6%)
  between operations  14.9 us (2%)
  starting transfers between devices  14.4 us (1%)
    all_gather x1, blocking collectives, on_device(): lax.all_gather(tile_sends[0], 'brick', axis=1, tiled=True)  404 us
    psum x1, waiting for transfers between devices, on_device(): lax.psum((part_w_in, part_w_out), ('drive', 'brick'))  253 us
    gather x12, local copies, waits for them, and re-layouts, attend(): keyval[jnp.maximum(entry_block, 0)]  77.1 us
    sub x6, other arithmetic, attend(): raised = jnp.exp(scores - row_peak)  52.4 us
    reshape x6, local copies, waits for them, and re-layouts, attend(): keyval[jnp.maximum(entry_block, 0)]  40.4 us
    dot_general x6, matrix products, attend(): jnp.einsum('gqhd,gkhd->ghqk', query_block, keys_part, preferred_element_t...  27.1 us
  transfers between devices with their start and end apart: 3, of which 1 were waited for; matrix products, arithmetic and copies ran while one was open for 2% of the time, Pallas kernels for 0%

profile of v1, /device:TPU:2, one launch (start us, length us, event | category | flops | bytes accessed | tf_op | source)
XLA Modules:
  0.0 986.7 jit_solution(7081520909274607711)
XLA Ops:
  14.6 12.4 %all-to-all-start = ((bf16[64,1,4,64,512]{4,3,2,1,0:T(8,128)(2,1)}), bf16[64,1,4,64,512]{4,3,2,1,0:T(8,128)(2,1)}, u32[]{:S(2)}, u32[]{:S(2)}) async-start(bf16[64,1,4,64,512]{4,3,2,1,0:T(8,128)(2,1)} %stack.3), calls=%async_computation | async-start | bytes 33554432 | tf_op jit(solution)/shard_map/all_to_all | solution.py:66
  29.7 404.4 %all-gather = s32[1,64,1,128]{3,2,0,1:T(1,128)S(1)} all-gather(s32[1,1,1,128]{3,2,0,1:T(1,128)S(1)} %bitcast.77), channel_id=2, replica_groups=mesh['drive'=4,'brick'=64] {'brick'}, dimensions={1}, use_global_device_ids=true | all-gather | bytes 33280 | tf_op jit(solution)/shard_map/all_gather | solution.py:68
  446.2 12.5 %gather_fusion.1 = bf16[128,64,512]{2,1,0:T(8,128)(2,1)} fusion(bf16[1,256,64,512]{3,2,1,0:T(8,128)(2,1)} %bitcast.13, s32[128]{0:T(128)S(1)} %or_bitcast_fusion), kind=kCustom, calls=%fused_computation.1 | custom fusion | bytes 16778240 | tf_op jit(solution)/shard_map/vmap()/gather | solution.py:25
  458.7 236.0 %while.10 = (s32[]{:T(128)}, bf16[6,4,128,8,32]{2,1,0,4,3:T(4,128)(2,1)}, s32[6,4,8]{2,1,0:T(4,128)S(1)}, bf16[128,64,512]{2,1,0:T(8,128)(2,1)}, bf16[6,4,128,8,32]{2,1,0,4,3:T(4,128)(2,1)}, /*index=5*/s32[]{:T(128)}) while((s32[]{:T(128)}, bf16[6,4,128,8,32]{2,1,0,4,3:T(4,128)(2,1)}, s32[6,4,8]{2,1,0:T(4,128)S(1)}, ...), condition=%wide.region_4.5_spmd, body=%wide.region_1.4_spmd.sunk | while | flops 285345344 | bytes 54048272 | solution.py:114
  464.2 7.4 copy.60
  471.6 6.7 reshape.157
  486.4 8.7 fusion.54
  503.5 7.4 copy.60
  511.0 6.7 reshape.157
  525.7 8.7 fusion.54
  542.9 7.4 copy.60
  550.3 6.7 reshape.157
  565.0 8.7 fusion.54
  582.2 7.4 copy.60
  589.6 6.7 reshape.157
  604.4 8.7 fusion.54
  621.5 7.4 copy.60
  629.0 6.7 reshape.157
  643.7 8.7 fusion.54
  660.9 7.4 copy.60
  668.3 6.7 reshape.157
  683.0 8.7 fusion.54
  708.4 9.6 fusion.19
  723.1 253.0 %all-reduce.3.cloned.1.call-done = (f32[256,512]{1,0:T(8,128)}, f32[512,256]{1,0:T(8,128)}) async-done(((f32[256,512]{1,0:T(8,128)}, f32[512,256]{1,0:T(8,128)}), (f32[256,512]{1,0:T(8,128)}, f32[512,256]{1,0:T(8,128)})) %all-reduce.3.cloned.1.call-update) | async-done | bytes 1048592 | tf_op jit(solution)/shard_map/psum | solution.py:134
  (129 shorter events, 142.4 us)
Async XLA Ops:
  7.2 697.8 %copy-start = (bf16[1,24,128,256]{3,2,1,0:T(8,128)(2,1)S(1)}, bf16[1,24,128,256]{3,2,1,0:T(8,128)(2,1)}, u32[]{:S(2)}) copy-start(bf16[1,24,128,256]{3,2,1,0:T(8,128)(2,1)} %param.27) | copy-start | bytes 4718596
  14.6 12.4 %copy-start.4 = (bf16[1,24,128,256]{3,2,1,0:T(8,128)(2,1)S(1)}, bf16[1,24,128,256]{3,2,1,0:T(8,128)(2,1)}, u32[]{:S(2)}) copy-start(bf16[1,24,128,256]{3,2,1,0:T(8,128)(2,1)} %param.17) | copy-start | bytes 4718596
  14.6 15.1 %copy-start.10 = (s32[1,1,1,128]{3,2,1,0:T(1,128)S(1)}, s32[1,1,1,128]{3,2,1,0:T(1,128)}, u32[]{:S(2)}) copy-start(s32[1,1,1,128]{3,2,1,0:T(1,128)} %param.18) | copy-start | bytes 1540
  14.6 420.0 %copy-start.8 = (s32[1,1,24,8]{2,3,1,0:T(8,128)S(1)}, s32[1,1,24,8]{2,3,1,0:T(8,128)}, u32[]{:S(2)}) copy-start(s32[1,1,24,8]{2,3,1,0:T(8,128)} %param.19) | copy-start | bytes 2308
  14.6 420.2 %copy-start.9 = (f32[2,256]{1,0:T(2,128)S(1)}, f32[2,256]{1,0:T(2,128)}, u32[]{:S(2)}) copy-start(f32[2,256]{1,0:T(2,128)} %param.21) | copy-start | bytes 6148
  14.6 431.6 %all-to-all-start = ((bf16[64,1,4,64,512]{4,3,2,1,0:T(8,128)(2,1)}), bf16[64,1,4,64,512]{4,3,2,1,0:T(8,128)(2,1)}, u32[]{:S(2)}, u32[]{:S(2)}) async-start(bf16[64,1,4,64,512]{4,3,2,1,0:T(8,128)(2,1)} %stack.3), calls=%async_computation | async-start | bytes 33554432 | tf_op jit(solution)/shard_map/all_to_all | solution.py:66
  26.9 949.2 %all-reduce.3.cloned.1.call-start = ((), (), s32[]{:S(2)}) async-start(), calls=%async_computation.1 | async-start | bytes 2097152 | tf_op jit(solution)/shard_map/psum | solution.py:134
  27.0 407.8 %collective-permute-start = (bf16[24,128,256]{2,1,0:T(8,128)(2,1)S(1)}, bf16[24,128,256]{2,1,0:T(8,128)(2,1)}, u32[]{:S(2)}, u32[]{:S(2)}) collective-permute-start(bf16[24,128,256]{2,1,0:T(8,128)(2,1)S(1)} %bitcast.69), channel_id=1, source_target_pairs={{0,1},{1,2},{2,3},{3,4},{4,5},{5,6},{6,7},{7,8},{8,9},{9,10},{10,1... | collective-permute-start | bytes 4718600 | tf_op jit(solution)/shard_map/ppermute | solution.py:12
  437.4 1.6 copy-start.1
  437.4 2.1 copy-start.7
  694.7 2.9 copy-start.6
  697.6 3.1 copy-start.11
  700.6 4.3 copy-start.2
  705.0 1.6 copy-start.3
  705.0 3.5 copy-start.5
Sparse Core Ops, SparseCore 0:
  718.2 257.8 all-reduce.2
